TPU v7x, 512 devices: a whole 4x4x16 slice. The times are simulated.
512 devices in a mesh: ctx: 64 (over y, z_hi, x, core), tp: 8 (over z_lo).
Axes of the slice: x: 4, y: 4, z: 16 (z_hi: 2, z_lo: 8; z = z_hi * 8 + z_lo), core: 2. Of those that a mesh axis runs over, the one named last changes fastest.
Arguments:
- hyena_in: bfloat16 [16384, 3, 4096], P('ctx', None, 'tp'), may hold values from -6 to 6
- filters: float32 [128, 4096], P(None, 'tp'), may hold values from -0.5 to 0.5
- attn_in: bfloat16 [16384, 3, 4096], P('ctx', None, 'tp'), may hold values from -18.5 to 18.5
- out_weight: bfloat16 [4096, 4096], P('tp', 'ctx'), may hold values from -0.25 to 0.25
- attn_weight: bfloat16 [4096, 4096], P('tp', 'ctx'), may hold values from -0.25 to 0.25
Outputs:
- block_out: bfloat16 [16384, 4096], P('ctx', 'tp')
- attn_block: bfloat16 [16384, 4096], P('ctx', 'tp')
All inputs are finite; a program needn't handle non-finite values.
Results may differ from a plain program's by a relative error of at most 0.014.
Values may be sent and summed in bfloat16 or wider, within the bound.
A program may use at most 64 MiB of HBM per device.

v0:
```python
import functools
import math

import jax
import jax.numpy as jnp
from jax import lax
from jax.experimental import pallas as pl
from jax.experimental.pallas import tpu as pltpu
from jax.sharding import PartitionSpec as P

HEAD_DIM = 128
WINDOW = 2048
GROUPS = 2
F32 = jnp.float32
BF16 = jnp.bfloat16


def kernel(
    window,
    hyena,
    filters,
    attn,
    w_hyena,
    w_attn,
    out_h,
    out_a,
    kv,
    wg,
    part,
    from_left,
    from_right,
    rim,
    padded,
    shifted,
    act,
    scores,
    kv_recv,
    kv_send,
    w_recv,
    w_send,
    rs_recv,
    rs_send,
    rim_recv,
    rim_send,
):
    _, rows, width = attn.shape
    heads = width // HEAD_DIM
    taps = filters.shape[0]
    n_ctx = lax.axis_size("ctx")
    n_tp = lax.axis_size("tp")
    slots = window // rows
    n_x = slots // 2
    n_y = n_ctx // (2 * slots)
    piece = w_hyena.shape[0]
    pair = 2 * piece
    row_w = slots * piece
    dest_w = out_h.shape[1]
    half = rows // GROUPS

    me = lax.axis_index("ctx")
    t = lax.axis_index("tp")
    row = me // slots
    i = me % slots
    y = row // 2
    zh = row % 2
    x = i // 2
    k = i % 2
    n_rows = n_ctx // slots

    def at(y_, zh_, x_, k_):
        return ((y_ * 2 + zh_) * n_x + x_) * 2 + k_

    partner = at(y, zh, x, 1 - k)
    flip = at(y, 1 - zh, x, k)
    row_next = lax.rem(row + 1, n_rows) * slots + i
    row_prev = lax.rem(row + n_rows - 1, n_rows) * slots + i
    after = lax.rem(me + 1, n_ctx)
    before = lax.rem(me + n_ctx - 1, n_ctx)
    x_peer = [at(y, zh, lax.rem(x + d, n_x), k) for d in range(1, n_x)]
    y_peer = [at(lax.rem(y + d, n_y), zh, x, k) for d in range(1, n_y)]

    barrier = pltpu.get_barrier_semaphore()
    peers = [partner, flip, row_next, row_prev, after, before] + x_peer + y_peer
    for peer in peers:
        pl.semaphore_signal(barrier, inc=1, device_id={"ctx": peer})

    @pl.when(t > 0)
    def _():
        pl.semaphore_signal(barrier, inc=1, device_id={"tp": t - 1})

    @pl.when(t < n_tp - 1)
    def _():
        pl.semaphore_signal(barrier, inc=1, device_id={"tp": t + 1})

    beside = (t > 0).astype(jnp.int32) + (t < n_tp - 1).astype(jnp.int32)
    pl.semaphore_wait(barrier, len(peers) + beside)

    def remote(src, dst, send, recv, peer, axis="ctx"):
        return pltpu.make_async_remote_copy(
            src_ref=src, dst_ref=dst, send_sem=send, recv_sem=recv, device_id={axis: peer}
        )

    def lanes(h):
        return pl.ds(pl.multiple_of(h * HEAD_DIM, HEAD_DIM), HEAD_DIM)

    def own_kv(h):
        return attn.at[pl.ds(1, 2), :, lanes(h)]

    def slot_kv(j, h):
        return kv.at[:, j, :, lanes(h)]

    def kv_copy(src, h, j, n, peer):
        return remote(src, slot_kv(j, h), kv_send.at[h, n], kv_recv.at[h, j], peer)

    def flip_kv(h):
        return kv_copy(own_kv(h), h, i, 0, row_next)

    def along(h, d, src):
        return kv_copy(src, h, i, d, x_peer[d - 1])

    def to_partner(h, src):
        return kv_copy(src, h, i, n_x, partner)

    def came(d):
        return lax.rem(x + d, n_x) * 2 + k

    def forward(h, d):
        j = came(d)
        return kv_copy(slot_kv(j, h), h, j, n_x + d, partner)

    def start_own(h):
        for d in range(1, n_x):

            @pl.when(x + d < n_x)
            def _():
                along(h, d, own_kv(h)).start()

        @pl.when(k == 0)
        def _():
            to_partner(h, own_kv(h)).start()

    def arrived(h, j):
        pltpu.make_async_copy(slot_kv(j, h), slot_kv(j, h), kv_recv.at[h, j]).wait()

    def spread(h):
        arrived(h, i)
        for d in range(1, n_x):

            @pl.when(x + d >= n_x)
            def _():
                along(h, d, slot_kv(i, h)).start()

        @pl.when(k == 1)
        def _():
            to_partner(h, slot_kv(i, h)).start()

    def pass_on(h):
        for d in range(1, n_x):
            arrived(h, came(d))
            forward(h, d).start()

    def rest(h):
        for d in range(n_x):
            arrived(h, lax.rem(x + d, n_x) * 2 + 1 - k)

    def w_rows(first, count):
        return pl.ds(pl.multiple_of(first * piece, piece), count * piece)

    def w_block(layer, first, count):
        return wg.at[layer, w_rows(first, count)]

    def w_copy(block, n, peer):
        return remote(block, block, w_send.at[n], w_recv.at[n], peer)

    def w_swap(src):
        return remote(src, w_block(1 - k, me, 1), w_send.at[0], w_recv.at[0], partner)

    def w_landed(block, n):
        pltpu.make_async_copy(block, block, w_recv.at[n]).wait()

    chip = me - k
    chip_flip = flip - k

    def w_own(ref):
        return pltpu.make_async_copy(ref, w_block(k, me, 1), w_recv.at[1])

    def w_flip():
        return w_copy(w_block(k, chip, 2), 2, flip)

    def w_along(d, other):
        return w_copy(
            w_block(k, chip_flip if other else chip, 2), 2 + d + (n_x - 1) * other, x_peer[d - 1]
        )

    base_y = 2 + 2 * n_x - 1

    def w_up(d):
        return w_copy(w_block(k, y * 2 * slots, 2 * slots), base_y + d, y_peer[d - 1])

    base_p = base_y + n_y

    def w_hand(d):
        y_ = lax.rem(y + d, n_y)
        block = w_block(k, y_ * 2 * slots, 2 * slots)
        return w_copy(block, base_p + d, partner)

    flip_kv(0).start()
    rim_rows = pl.ds(rows - taps, taps)
    for n in range(2):
        remote(hyena.at[2 * n, rim_rows], rim.at[n], rim_send.at[n], rim_recv.at[n], after).start()

    @pl.when(k == 0)
    def _():
        w_swap(w_attn).start()
        w_own(w_hyena).start()

    @pl.when(k == 1)
    def _():
        w_swap(w_hyena).start()
        w_own(w_attn).start()

    start_own(0)
    w_landed(w_block(k, me, 1), 1)
    w_landed(w_block(k, partner, 1), 0)
    w_flip().start()
    for d in range(1, n_x):
        w_along(d, 0).start()

    @pl.loop(1, heads)
    def _(h):
        flip_kv(h).start()
        start_own(h)

    own = (hyena[0].astype(F32) * hyena[2].astype(F32)).astype(BF16).astype(F32)
    padded[pl.ds(taps, rows), :] = own
    for n in range(2):
        pltpu.make_async_copy(rim.at[n], rim.at[n], rim_recv.at[n]).wait()
    rim_product = (rim[0].astype(F32) * rim[1].astype(F32)).astype(BF16).astype(F32)
    padded[pl.ds(0, taps), :] = jnp.where(me > 0, rim_product, 0.0)

    total_rows = taps + rows

    @pl.loop(0, width // 128)
    def _(tile):
        cols = pl.ds(pl.multiple_of(tile * 128, 128), 128)
        for s in range(8):
            shifted[s, pl.ds(8, total_rows - 8), :] = padded[pl.ds(8 - s, total_rows - 8), cols]

        chunk = min(rows, 128)

        @pl.loop(0, rows // chunk)
        def _(part_row):
            first = part_row * chunk

            def eight(a, acc):
                coef = filters[pl.ds(pl.multiple_of(a * 8, 8), 8), cols]
                start = pl.multiple_of(taps + first - a * 8, 8)
                for s in range(8):
                    acc = acc + coef[s : s + 1, :] * shifted[s, pl.ds(start, chunk), :]
                return acc

            acc = lax.fori_loop(0, taps // 8, eight, jnp.zeros((chunk, 128), F32))
            at_rows = pl.ds(pl.multiple_of(first, chunk), chunk)
            act[at_rows, cols] = (hyena[1, at_rows, cols].astype(F32) * acc).astype(BF16)

    w_landed(w_block(k, chip_flip, 2), 2)
    for d in range(1, n_x):
        w_along(d, 1).start()
    spread(0)
    for d in range(1, n_x):
        x_ = lax.rem(x + n_x - d, n_x)
        w_landed(w_block(k, at(y, zh, x_, 0), 2), 2 + d)
    for d in range(1, n_x):
        x_ = lax.rem(x + n_x - d, n_x)
        w_landed(w_block(k, at(y, 1 - zh, x_, 0), 2), 2 + d + n_x - 1)
    for d in range(1, n_y):
        w_up(d).start()
    w_hand(0).start()
    pass_on(0)

    @pl.loop(1, heads)
    def _(h):
        spread(h)
        pass_on(h)

    for d in range(1, n_y):
        y_ = lax.rem(y + n_y - d, n_y)
        w_landed(w_block(k, y_ * 2 * slots, 2 * slots), base_y + d)
        w_hand(n_y - d).start()
    for d in range(n_y):
        y_ = lax.rem(y + d, n_y)
        w_landed(w_block(1 - k, y_ * 2 * slots, 2 * slots), base_p + d)

    def project(layer):
        @pl.loop(0, n_tp)
        def _(d):
            weight = wg[layer, pl.ds(pl.multiple_of(d * dest_w, dest_w), dest_w), :]
            part[layer, d] = lax.dot_general(
                act[...], weight, (((1,), (1,)), ((), ())), preferred_element_type=F32
            ).astype(BF16)

    def rs_copy(layer, way, d, g):
        piece_of = (d, pl.ds(pl.multiple_of(g * half, half), half))
        buffer = (from_left, from_right)[way]
        return remote(
            part.at[(layer,) + piece_of],
            buffer.at[(layer,) + piece_of],
            rs_send.at[layer, way, d, g],
            rs_recv.at[layer, way, d, g],
            (t + 1, t - 1)[way],
            "tp",
        )

    def rs_add(layer, way, d, g):
        piece_of = (layer, d, pl.ds(pl.multiple_of(g * half, half), half))
        buffer = (from_left, from_right)[way]
        landed = buffer.at[piece_of]
        pltpu.make_async_copy(landed, landed, rs_recv.at[layer, way, d, g]).wait()
        part[piece_of] = (part[piece_of].astype(F32) + buffer[piece_of].astype(F32)).astype(BF16)

    def rs_step(layer, step):
        m = step // GROUPS
        g = step % GROUPS
        right = n_tp - 1 - m
        left = m

        @pl.when((t < right) & (t > 0))
        def _():
            rs_add(layer, 0, right, g)

        @pl.when(t < right)
        def _():
            rs_copy(layer, 0, right, g).start()

        @pl.when((t > left) & (t < n_tp - 1))
        def _():
            rs_add(layer, 1, left, g)

        @pl.when(t > left)
        def _():
            rs_copy(layer, 1, left, g).start()

    rs_steps = (n_tp - 1) * GROUPS

    def finish(layer, out):
        total = part[layer, t].astype(F32)
        for way in range(2):

            @pl.when((t > 0) if way == 0 else (t < n_tp - 1))
            def _():
                for g in range(GROUPS):
                    buffer = (from_left, from_right)[way]
                    landed = buffer.at[layer, t, pl.ds(g * half, half)]
                    pltpu.make_async_copy(landed, landed, rs_recv.at[layer, way, t, g]).wait()

        left = jnp.where(t > 0, from_left[layer, t].astype(F32), 0.0)
        right = jnp.where(t < n_tp - 1, from_right[layer, t].astype(F32), 0.0)
        out[...] = (total + left + right).astype(BF16)

    project(0)

    scale = 1.0 / math.sqrt(HEAD_DIM)
    gap = lax.broadcasted_iota(jnp.int32, (rows, rows), 1) - lax.broadcasted_iota(
        jnp.int32, (rows, rows), 0
    )

    def attend(h):
        queries = attn[0, :, lanes(h)]

        def block_scores(keys):
            return (
                lax.dot_general(
                    queries, keys, (((1,), (1,)), ((), ())), preferred_element_type=F32
                )
                * scale
            )

        def fold(op, block):
            kept = block[:, :128]
            for n in range(1, rows // 128):
                kept = op(kept, block[:, n * 128 : (n + 1) * 128])
            return kept

        own = jnp.where(gap <= 0, block_scores(attn[1, :, lanes(h)]), -jnp.inf)
        scores[:, slots * rows :] = own
        top = fold(jnp.maximum, own)
        for j in range(slots):
            least = jnp.where(i == j, 0, -rows)
            least = jnp.where((row == 0) & (i <= j), rows, least)
            block = jnp.where(gap > least, block_scores(kv[0, j, :, lanes(h)]), -jnp.inf)
            scores[:, j * rows : (j + 1) * rows] = block
            top = jnp.maximum(top, fold(jnp.maximum, block))
        top = jnp.max(top, axis=1, keepdims=True)
        total = jnp.zeros((rows, 128), F32)
        result = jnp.zeros((rows, HEAD_DIM), F32)
        for j in range(slots + 1):
            weights = jnp.exp(scores[:, j * rows : (j + 1) * rows] - top)
            total = total + fold(jnp.add, weights)
            values = attn[2, :, lanes(h)] if j == slots else kv[1, j, :, lanes(h)]
            result = result + jnp.dot(weights.astype(BF16), values, preferred_element_type=F32)
        total = jnp.sum(total, axis=1, keepdims=True)
        act[:, lanes(h)] = (result / total).astype(BF16)

    per_head = -(-rs_steps // heads)

    @pl.loop(0, heads)
    def _(h):
        rest(h)
        attend(h)

        @pl.loop(h * per_head, jnp.minimum((h + 1) * per_head, rs_steps))
        def _(step):
            rs_step(0, step)

    project(1)

    @pl.loop(0, rs_steps)
    def _(step):
        rs_step(1, step)

    finish(0, out_h)
    finish(1, out_a)

    for n in range(2):
        remote(hyena.at[2 * n, rim_rows], rim.at[n], rim_send.at[n], rim_recv.at[n], after).wait_send()
    w_swap(w_attn).wait_send()
    w_flip().wait_send()
    for d in range(1, n_x):
        w_along(d, 0).wait_send()
        w_along(d, 1).wait_send()
    for d in range(1, n_y):
        w_up(d).wait_send()
    for d in range(n_y):
        w_hand(d).wait_send()

    @pl.loop(0, heads)
    def _(h):
        flip_kv(h).wait_send()
        for d in range(1, n_x):
            along(h, d, own_kv(h)).wait_send()
            forward(h, d).wait_send()
        to_partner(h, own_kv(h)).wait_send()

    @pl.loop(0, rs_steps)
    def _(step):
        m = step // GROUPS
        g = step % GROUPS
        for layer in range(2):

            @pl.when(t < n_tp - 1 - m)
            def _():
                rs_copy(layer, 0, n_tp - 1 - m, g).wait_send()

            @pl.when(t > m)
            def _():
                rs_copy(layer, 1, m, g).wait_send()


def per_device(window, n_tp, hyena_in, filters, attn_in, out_weight, attn_weight):
    hyena = hyena_in.transpose(1, 0, 2)
    attn = attn_in.transpose(1, 0, 2)
    _, rows, width = attn.shape
    taps = filters.shape[0]
    piece = out_weight.shape[1]
    n_ctx = lax.axis_size("ctx")
    slots = window // rows
    n_x = slots // 2
    n_y = n_ctx // (2 * slots)
    columns = piece * n_ctx
    dest_w = columns // n_tp
    heads = width // HEAD_DIM
    n_w = 2 + 2 * n_x + 2 * n_y
    dma = pltpu.SemaphoreType.DMA
    result = jax.ShapeDtypeStruct((rows, dest_w), BF16)
    return pl.pallas_call(
        functools.partial(kernel, window),
        out_shape=(result, result),
        in_specs=[pl.BlockSpec(memory_space=pltpu.VMEM)] * 5,
        out_specs=(pl.BlockSpec(memory_space=pltpu.VMEM),) * 2,
        scratch_shapes=[
            pltpu.VMEM((2, slots, rows, width), BF16),
            pltpu.VMEM((2, columns, width), BF16),
            pltpu.VMEM((2, n_tp, rows, dest_w), BF16),
            pltpu.VMEM((2, n_tp, rows, dest_w), BF16),
            pltpu.VMEM((2, n_tp, rows, dest_w), BF16),
            pltpu.VMEM((2, taps, width), BF16),
            pltpu.VMEM((taps + rows, width), F32),
            pltpu.VMEM((8, taps + rows, 128), F32),
            pltpu.VMEM((rows, width), BF16),
            pltpu.VMEM((rows, (slots + 1) * rows), F32),
            dma((heads, slots)),
            dma((heads, 2 * n_x)),
            dma((n_w,)),
            dma((n_w,)),
            dma((2, 2, n_tp, GROUPS)),
            dma((2, 2, n_tp, GROUPS)),
            dma((2,)),
            dma((2,)),
        ],
        compiler_params=pltpu.CompilerParams(
            collective_id=0, has_side_effects=True, vmem_limit_bytes=60 * 2**20
        ),
    )(hyena, filters, attn, out_weight.T, attn_weight.T)


def build(mesh, window):
    in_specs = (
        P("ctx", None, "tp"),
        P(None, "tp"),
        P("ctx", None, "tp"),
        P("tp", "ctx"),
        P("tp", "ctx"),
    )
    return jax.shard_map(
        functools.partial(per_device, window, mesh.shape["tp"]),
        mesh=mesh,
        in_specs=in_specs,
        out_specs=(P("ctx", "tp"), P("ctx", "tp")),
        check_vma=False,
    )


def solution(mesh):
    return build(mesh, WINDOW)
```

profile of v0, /device:TPU:70, one launch (start us, length us, event | category | flops | bytes accessed | tf_op | source)
XLA Modules:
  0.0 479.8 jit_solution(6973671736930793883)
XLA Ops:
  0.6 476.7 %shard_map.68 = (bf16[256,512]{1,0:T(8,128)(2,1)}, bf16[256,512]{1,0:T(8,128)(2,1)}) custom-call(bf16[3,256,512]{2,1,0:T(8,128)(2,1)} %bitcast.4, f32[128,512]{1,0:T(8,128)} %filters.1, bf16[3,256,512]{2,1,0:T(8,128)(2,1)} %bitcast.5, bf16[64,512]{1,0:T(8,128)(2,1)} %bitcast.6, bf16[64,512]{1,0:T(8,128)(2,1)} %bitcast.7), custom_call_target="tpu_custom_call" | custom-call | tf_op jit(solution)/shard_map/pallas_call | solution.py:475
  477.4 0.0 copy-start
  477.4 1.7 copy.9
  479.1 0.0 copy-done
  479.1 0.7 copy.10
Async XLA Ops:
  477.4 1.7 copy-start
where the time goes:
time: 480 us
  Pallas kernels  477 us (99%)
    pallas_call x1, Pallas kernels, per_device(): pl.pallas_call(functools.partial(kernel, window), out_shape=(result, resu...  477 us

commit v1 on v0

--- a/solution.py
+++ b/solution.py
@@ -318,27 +318,26 @@
         pltpu.make_async_copy(landed, landed, rs_recv.at[layer, way, d, g]).wait()
         part[piece_of] = (part[piece_of].astype(F32) + buffer[piece_of].astype(F32)).astype(BF16)
 
-    def rs_step(layer, step):
+    def rs_way(layer, way, tick):
+        hops = (t, n_tp - 1 - t)[way]
+        step = tick - hops
+        count = (n_tp - 1 - hops) * GROUPS
         m = step // GROUPS
+        d = (n_tp - 1 - m, m)[way]
         g = step % GROUPS
-        right = n_tp - 1 - m
-        left = m
-
-        @pl.when((t < right) & (t > 0))
+        live = (step >= 0) & (step < count)
+
+        @pl.when(live & (hops > 0))
         def _():
-            rs_add(layer, 0, right, g)
-
-        @pl.when(t < right)
+            rs_add(layer, way, d, g)
+
+        @pl.when(live)
         def _():
-            rs_copy(layer, 0, right, g).start()
-
-        @pl.when((t > left) & (t < n_tp - 1))
-        def _():
-            rs_add(layer, 1, left, g)
-
-        @pl.when(t > left)
-        def _():
-            rs_copy(layer, 1, left, g).start()
+            rs_copy(layer, way, d, g).start()
+
+    def rs_step(layer, tick):
+        rs_way(layer, 0, tick)
+        rs_way(layer, 1, tick)
 
     rs_steps = (n_tp - 1) * GROUPS
 

time: 480 us -> 232 us (0.48)
  the two profiles are of different devices: /device:TPU:70 before, /device:TPU:96 now
where the time goes in v1:
time: 232 us
  Pallas kernels  228 us (98%)
  local copies, waits for them, and re-layouts  2.42 us (1%)
    pallas_call x1, Pallas kernels, per_device(): pl.pallas_call(functools.partial(kernel, window), out_shape=(result, resu...  228 us

profile of v1, /device:TPU:96, one launch (start us, length us, event | category | flops | bytes accessed | tf_op | source)
XLA Modules:
  0.0 231.5 jit_solution(1658016901075560149)
XLA Ops:
  0.6 228.5 %shard_map.68 = (bf16[256,512]{1,0:T(8,128)(2,1)}, bf16[256,512]{1,0:T(8,128)(2,1)}) custom-call(bf16[3,256,512]{2,1,0:T(8,128)(2,1)} %bitcast.4, f32[128,512]{1,0:T(8,128)} %filters.1, bf16[3,256,512]{2,1,0:T(8,128)(2,1)} %bitcast.5, bf16[64,512]{1,0:T(8,128)(2,1)} %bitcast.6, bf16[64,512]{1,0:T(8,128)(2,1)} %bitcast.7), custom_call_target="tpu_custom_call" | custom-call | tf_op jit(solution)/shard_map/pallas_call | solution.py:474
  229.1 0.0 copy-start
  229.1 1.7 copy.9
  230.8 0.0 copy-done
  230.8 0.7 copy.10
Async XLA Ops:
  229.1 1.7 copy-start

commit v2 on v1

--- a/solution.py
+++ b/solution.py
@@ -26,9 +26,14 @@
     out_a,
     kv,
     wg,
+    w_far,
+    w_share,
+    wa,
+    gathered,
     part,
     from_left,
     from_right,
+    rim_out,
     rim,
     padded,
     shifted,
@@ -42,6 +47,10 @@
     rs_send,
     rim_recv,
     rim_send,
+    wa_recv,
+    wa_send,
+    ag_recv,
+    ag_send,
 ):
     _, rows, width = attn.shape
     heads = width // HEAD_DIM
@@ -93,7 +102,19 @@
         pl.semaphore_signal(barrier, inc=1, device_id={"tp": t + 1})
 
     beside = (t > 0).astype(jnp.int32) + (t < n_tp - 1).astype(jnp.int32)
-    pl.semaphore_wait(barrier, len(peers) + beside)
+
+    holder = t % 2 == zh
+
+    @pl.when(holder)
+    def _():
+        for s in range(n_tp):
+
+            @pl.when(s != t)
+            def _():
+                pl.semaphore_signal(barrier, inc=1, device_id={"tp": s})
+
+    collectors = n_tp // 2 - holder.astype(jnp.int32)
+    pl.semaphore_wait(barrier, len(peers) + beside + collectors)
 
     def remote(src, dst, send, recv, peer, axis="ctx"):
         return pltpu.make_async_remote_copy(
@@ -163,17 +184,27 @@
         for d in range(n_x):
             arrived(h, lax.rem(x + d, n_x) * 2 + 1 - k)
 
+    side_w = width // 2
+
+    def side(k_):
+        return pl.ds(pl.multiple_of(k_ * side_w, side_w), side_w)
+
     def w_rows(first, count):
         return pl.ds(pl.multiple_of(first * piece, piece), count * piece)
 
-    def w_block(layer, first, count):
-        return wg.at[layer, w_rows(first, count)]
+    def w_block(k_, first, count):
+        return wg.at[w_rows(first, count), side(k_)]
 
     def w_copy(block, n, peer):
         return remote(block, block, w_send.at[n], w_recv.at[n], peer)
 
-    def w_swap(src):
-        return remote(src, w_block(1 - k, me, 1), w_send.at[0], w_recv.at[0], partner)
+    def w_swap(src, owner, n):
+        return remote(
+            src.at[:, side(1 - k)], w_block(1 - k, owner, 1), w_send.at[n], w_recv.at[n], partner
+        )
+
+    def w_keep(src, owner, n):
+        return pltpu.make_async_copy(src.at[:, side(k)], w_block(k, owner, 1), w_recv.at[n])
 
     def w_landed(block, n):
         pltpu.make_async_copy(block, block, w_recv.at[n]).wait()
@@ -181,11 +212,10 @@
     chip = me - k
     chip_flip = flip - k
 
-    def w_own(ref):
-        return pltpu.make_async_copy(ref, w_block(k, me, 1), w_recv.at[1])
+    last = 2 + 2 * n_x + 2 * n_y
 
     def w_flip():
-        return w_copy(w_block(k, chip, 2), 2, flip)
+        return remote(w_hyena, w_far, w_send.at[2], w_recv.at[2], flip)
 
     def w_along(d, other):
         return w_copy(
@@ -204,53 +234,148 @@
         block = w_block(k, y_ * 2 * slots, 2 * slots)
         return w_copy(block, base_p + d, partner)
 
-    flip_kv(0).start()
-    rim_rows = pl.ds(rows - taps, taps)
-    for n in range(2):
-        remote(hyena.at[2 * n, rim_rows], rim.at[n], rim_send.at[n], rim_recv.at[n], after).start()
-
-    @pl.when(k == 0)
-    def _():
-        w_swap(w_attn).start()
-        w_own(w_hyena).start()
-
-    @pl.when(k == 1)
-    def _():
-        w_swap(w_hyena).start()
-        w_own(w_attn).start()
-
-    start_own(0)
-    w_landed(w_block(k, me, 1), 1)
-    w_landed(w_block(k, partner, 1), 0)
+    share = piece // n_y
+
+    def wa_part(j, y_):
+        return pl.ds(pl.multiple_of(j * piece + y_ * share, share), share)
+
+    def wa_block(j):
+        return wa.at[:, w_rows(j, 1)]
+
+    def wa_scatter(d):
+        y_ = lax.rem(y + d, n_y)
+        src = w_attn.at[pl.ds(pl.multiple_of(y_ * share, share), share)]
+        return remote(src, w_share.at[y], wa_send.at[d], wa_recv.at[y], y_peer[d - 1])
+
+    def wa_keep():
+        src = w_attn.at[pl.ds(pl.multiple_of(y * share, share), share)]
+        return pltpu.make_async_copy(src, w_share.at[y], wa_recv.at[y])
+
+    def wa_line(y_):
+        return remote(
+            w_share.at[y_],
+            wa.at[t, wa_part(i, y)],
+            wa_send.at[n_y + y_],
+            wa_recv.at[n_y + t],
+            2 * y_ + zh,
+            "tp",
+        )
+
+    def wa_own(y_):
+        return pltpu.make_async_copy(
+            w_share.at[y_], wa.at[t, wa_part(i, y)], wa_recv.at[n_y + t]
+        )
+
+    def wa_flip():
+        block = wa.at[:, wa_part(i, y)]
+        return remote(block, block, wa_send.at[2 * n_y], wa_recv.at[n_y + n_tp], flip)
+
+    def wa_up(d):
+        block = wa.at[:, wa_part(i, y)]
+        return remote(
+            block, block, wa_send.at[2 * n_y + d], wa_recv.at[n_y + n_tp + d], y_peer[d - 1]
+        )
+
+    def wa_along(d):
+        block = wa_block(i)
+        return remote(
+            block, block, wa_send.at[3 * n_y + d], wa_recv.at[2 * n_y + n_tp + d], x_peer[d - 1]
+        )
+
+    def wa_hand(d):
+        block = wa_block(lax.rem(x + d, n_x) * 2 + k)
+        n = n_x + d
+        return remote(
+            block, block, wa_send.at[3 * n_y + n], wa_recv.at[2 * n_y + n_tp + n], partner
+        )
+
+    def wa_landed(block, n):
+        pltpu.make_async_copy(block, block, wa_recv.at[n]).wait()
+
+    def wa_send_lines():
+        for y_ in range(n_y):
+            wa_landed(w_share.at[y_], y_)
+        for y_ in range(n_y):
+
+            @pl.when(2 * y_ + zh != t)
+            def _():
+                wa_line(y_).start()
+
+            @pl.when(2 * y_ + zh == t)
+            def _():
+                wa_own(y_).start()
+
+    def wa_collect():
+        @pl.when(holder)
+        def _():
+            for s in range(n_tp):
+                wa_landed(wa.at[s, wa_part(i, y)], n_y + s)
+            wa_flip().start()
+            for d in range(1, n_y):
+                wa_up(d).start()
+
+    def wa_spread():
+        @pl.when(jnp.logical_not(holder))
+        def _():
+            wa_landed(wa.at[:, wa_part(i, y)], n_y + n_tp)
+            for d in range(1, n_y):
+                wa_up(d).start()
+
+    def wa_rows_done():
+        for d in range(1, n_y):
+            wa_landed(wa.at[:, wa_part(i, lax.rem(y + n_y - d, n_y))], n_y + n_tp + d)
+        for d in range(1, n_x):
+            wa_along(d).start()
+        wa_hand(0).start()
+
+    def wa_hand_on():
+        for d in range(1, n_x):
+            j = lax.rem(x + n_x - d, n_x) * 2 + k
+            wa_landed(wa_block(j), 2 * n_y + n_tp + d)
+            wa_hand(n_x - d).start()
+
+    def wa_done():
+        for d in range(n_x):
+            j = lax.rem(x + d, n_x) * 2 + 1 - k
+            wa_landed(wa_block(j), 2 * n_y + n_tp + n_x + d)
+
+    product = (hyena[0].astype(F32) * hyena[2].astype(F32)).astype(BF16)
+    rim_out[...] = product[rows - taps :]
+
+    def rim_copy():
+        return remote(rim_out, rim, rim_send, rim_recv, after)
+
     w_flip().start()
-    for d in range(1, n_x):
-        w_along(d, 0).start()
-
-    @pl.loop(1, heads)
+    rim_copy().start()
+    w_swap(w_hyena, me, 0).start()
+    w_keep(w_hyena, me, 1).start()
+
+    for d in range(1, n_y):
+        wa_scatter(d).start()
+    wa_keep().start()
+
+    @pl.loop(0, heads)
     def _(h):
         flip_kv(h).start()
         start_own(h)
 
-    own = (hyena[0].astype(F32) * hyena[2].astype(F32)).astype(BF16).astype(F32)
-    padded[pl.ds(taps, rows), :] = own
-    for n in range(2):
-        pltpu.make_async_copy(rim.at[n], rim.at[n], rim_recv.at[n]).wait()
-    rim_product = (rim[0].astype(F32) * rim[1].astype(F32)).astype(BF16).astype(F32)
-    padded[pl.ds(0, taps), :] = jnp.where(me > 0, rim_product, 0.0)
-
-    total_rows = taps + rows
-
-    @pl.loop(0, width // 128)
-    def _(tile):
-        cols = pl.ds(pl.multiple_of(tile * 128, 128), 128)
-        for s in range(8):
-            shifted[s, pl.ds(8, total_rows - 8), :] = padded[pl.ds(8 - s, total_rows - 8), cols]
-
-        chunk = min(rows, 128)
-
-        @pl.loop(0, rows // chunk)
-        def _(part_row):
-            first = part_row * chunk
+    w_landed(w_block(k, me, 1), 1)
+    w_landed(w_block(k, partner, 1), 0)
+    for d in range(1, n_x):
+        w_along(d, 0).start()
+
+    padded[pl.ds(taps, rows), :] = product.astype(F32)
+    chunk = rows // 2
+
+    def convolve(first):
+        low = max(first - 8 * (taps // 8 - 1) + taps, 8)
+        count = first + taps + chunk - low
+
+        @pl.loop(0, width // 128)
+        def _(tile):
+            cols = pl.ds(pl.multiple_of(tile * 128, 128), 128)
+            for s in range(8):
+                shifted[s, pl.ds(low, count), :] = padded[pl.ds(low - s, count), cols]
 
             def eight(a, acc):
                 coef = filters[pl.ds(pl.multiple_of(a * 8, 8), 8), cols]
@@ -260,13 +385,19 @@
                 return acc
 
             acc = lax.fori_loop(0, taps // 8, eight, jnp.zeros((chunk, 128), F32))
-            at_rows = pl.ds(pl.multiple_of(first, chunk), chunk)
-            act[at_rows, cols] = (hyena[1, at_rows, cols].astype(F32) * acc).astype(BF16)
-
-    w_landed(w_block(k, chip_flip, 2), 2)
+            gate = hyena[1, pl.ds(first, chunk), cols].astype(F32)
+            act[pl.ds(first, chunk), cols] = (gate * acc).astype(BF16)
+
+    if chunk >= taps:
+        convolve(chunk)
+    wa_send_lines()
+    w_landed(w_far, 2)
+    w_swap(w_far, flip, last).start()
+    w_keep(w_far, flip, last + 1).start()
+    w_landed(w_block(k, flip, 1), last + 1)
+    w_landed(w_block(k, at(y, 1 - zh, x, 1 - k), 1), last)
     for d in range(1, n_x):
         w_along(d, 1).start()
-    spread(0)
     for d in range(1, n_x):
         x_ = lax.rem(x + n_x - d, n_x)
         w_landed(w_block(k, at(y, zh, x_, 0), 2), 2 + d)
@@ -276,49 +407,67 @@
     for d in range(1, n_y):
         w_up(d).start()
     w_hand(0).start()
-    pass_on(0)
-
-    @pl.loop(1, heads)
+    spread(0)
+
+    @pl.loop(0, heads // 2)
     def _(h):
-        spread(h)
+        spread(h + 1)
         pass_on(h)
 
     for d in range(1, n_y):
         y_ = lax.rem(y + n_y - d, n_y)
         w_landed(w_block(k, y_ * 2 * slots, 2 * slots), base_y + d)
         w_hand(n_y - d).start()
+
+    wa_collect()
+
+    @pl.loop(heads // 2, heads)
+    def _(h):
+        @pl.when(h < heads - 1)
+        def _():
+            spread(h + 1)
+
+        pass_on(h)
+
+    pltpu.make_async_copy(rim, rim, rim_recv).wait()
+    padded[pl.ds(0, taps), :] = jnp.where(me > 0, rim[...].astype(F32), 0.0)
+    convolve(0)
+    if chunk < taps:
+        convolve(chunk)
+
     for d in range(n_y):
         y_ = lax.rem(y + d, n_y)
         w_landed(w_block(1 - k, y_ * 2 * slots, 2 * slots), base_p + d)
 
-    def project(layer):
-        @pl.loop(0, n_tp)
-        def _(d):
-            weight = wg[layer, pl.ds(pl.multiple_of(d * dest_w, dest_w), dest_w), :]
-            part[layer, d] = lax.dot_general(
-                act[...], weight, (((1,), (1,)), ((), ())), preferred_element_type=F32
-            ).astype(BF16)
-
-    def rs_copy(layer, way, d, g):
+    @pl.loop(0, n_tp)
+    def _(d):
+        weight = wg[pl.ds(pl.multiple_of(d * dest_w, dest_w), dest_w), :]
+        part[d] = lax.dot_general(
+            act[...], weight, (((1,), (1,)), ((), ())), preferred_element_type=F32
+        ).astype(BF16)
+
+    wa_spread()
+
+    def rs_copy(way, d, g):
         piece_of = (d, pl.ds(pl.multiple_of(g * half, half), half))
         buffer = (from_left, from_right)[way]
         return remote(
-            part.at[(layer,) + piece_of],
-            buffer.at[(layer,) + piece_of],
-            rs_send.at[layer, way, d, g],
-            rs_recv.at[layer, way, d, g],
+            part.at[piece_of],
+            buffer.at[piece_of],
+            rs_send.at[way, d, g],
+            rs_recv.at[way, d, g],
             (t + 1, t - 1)[way],
             "tp",
         )
 
-    def rs_add(layer, way, d, g):
-        piece_of = (layer, d, pl.ds(pl.multiple_of(g * half, half), half))
+    def rs_add(way, d, g):
+        piece_of = (d, pl.ds(pl.multiple_of(g * half, half), half))
         buffer = (from_left, from_right)[way]
         landed = buffer.at[piece_of]
-        pltpu.make_async_copy(landed, landed, rs_recv.at[layer, way, d, g]).wait()
+        pltpu.make_async_copy(landed, landed, rs_recv.at[way, d, g]).wait()
         part[piece_of] = (part[piece_of].astype(F32) + buffer[piece_of].astype(F32)).astype(BF16)
 
-    def rs_way(layer, way, tick):
+    def rs_way(way, tick):
         hops = (t, n_tp - 1 - t)[way]
         step = tick - hops
         count = (n_tp - 1 - hops) * GROUPS
@@ -329,34 +478,32 @@
 
         @pl.when(live & (hops > 0))
         def _():
-            rs_add(layer, way, d, g)
+            rs_add(way, d, g)
 
         @pl.when(live)
         def _():
-            rs_copy(layer, way, d, g).start()
-
-    def rs_step(layer, tick):
-        rs_way(layer, 0, tick)
-        rs_way(layer, 1, tick)
+            rs_copy(way, d, g).start()
+
+    def rs_step(tick):
+        rs_way(0, tick)
+        rs_way(1, tick)
 
     rs_steps = (n_tp - 1) * GROUPS
 
-    def finish(layer, out):
-        total = part[layer, t].astype(F32)
+    def finish(out):
+        total = part[t].astype(F32)
         for way in range(2):
 
             @pl.when((t > 0) if way == 0 else (t < n_tp - 1))
             def _():
                 for g in range(GROUPS):
                     buffer = (from_left, from_right)[way]
-                    landed = buffer.at[layer, t, pl.ds(g * half, half)]
-                    pltpu.make_async_copy(landed, landed, rs_recv.at[layer, way, t, g]).wait()
-
-        left = jnp.where(t > 0, from_left[layer, t].astype(F32), 0.0)
-        right = jnp.where(t < n_tp - 1, from_right[layer, t].astype(F32), 0.0)
+                    landed = buffer.at[t, pl.ds(g * half, half)]
+                    pltpu.make_async_copy(landed, landed, rs_recv.at[way, t, g]).wait()
+
+        left = jnp.where(t > 0, from_left[t].astype(F32), 0.0)
+        right = jnp.where(t < n_tp - 1, from_right[t].astype(F32), 0.0)
         out[...] = (total + left + right).astype(BF16)
-
-    project(0)
 
     scale = 1.0 / math.sqrt(HEAD_DIM)
     gap = lax.broadcasted_iota(jnp.int32, (rows, rows), 1) - lax.broadcasted_iota(
@@ -398,31 +545,91 @@
             values = attn[2, :, lanes(h)] if j == slots else kv[1, j, :, lanes(h)]
             result = result + jnp.dot(weights.astype(BF16), values, preferred_element_type=F32)
         total = jnp.sum(total, axis=1, keepdims=True)
-        act[:, lanes(h)] = (result / total).astype(BF16)
-
-    per_head = -(-rs_steps // heads)
-
-    @pl.loop(0, heads)
-    def _(h):
-        rest(h)
-        attend(h)
-
-        @pl.loop(h * per_head, jnp.minimum((h + 1) * per_head, rs_steps))
-        def _(step):
-            rs_step(0, step)
-
-    project(1)
-
-    @pl.loop(0, rs_steps)
-    def _(step):
-        rs_step(1, step)
-
-    finish(0, out_h)
-    finish(1, out_a)
-
-    for n in range(2):
-        remote(hyena.at[2 * n, rim_rows], rim.at[n], rim_send.at[n], rim_recv.at[n], after).wait_send()
-    w_swap(w_attn).wait_send()
+        gathered[t, :, lanes(h)] = (result / total).astype(BF16)
+
+    def ag_copy(h, way, s):
+        block = gathered.at[s, :, lanes(h)]
+        return remote(
+            block, block, ag_send.at[h, way, s], ag_recv.at[h, s], (t + 1, t - 1)[way], "tp"
+        )
+
+    def ag_step(h, hops):
+        for way in range(2):
+            s = (t - hops, t + hops)[way]
+            live = (s >= 0, s < n_tp)[way]
+            more = (t < n_tp - 1, t > 0)[way]
+
+            @pl.when(live & (hops > 0))
+            def _():
+                block = gathered.at[s, :, lanes(h)]
+                pltpu.make_async_copy(block, block, ag_recv.at[h, s]).wait()
+
+            @pl.when(live & more)
+            def _():
+                ag_copy(h, way, s).start()
+
+    def add_source(s):
+        scores[:, :dest_w] += lax.dot_general(
+            gathered[s], wa[s], (((1,), (1,)), ((), ())), preferred_element_type=F32
+        )
+
+    def rs_pair(n):
+        @pl.loop(2 * n, jnp.minimum(2 * n + 2, rs_steps))
+        def _(tick):
+            rs_step(tick)
+
+    @pl.loop(0, heads // 2)
+    def _(n):
+        rest(n)
+        attend(n)
+
+        @pl.loop(0, n + 1)
+        def _(hops):
+            ag_step(n - hops, hops)
+
+        rs_pair(n)
+
+    wa_rows_done()
+
+    @pl.loop(heads // 2, heads)
+    def _(n):
+        rest(n)
+        attend(n)
+
+        @pl.loop(0, n + 1)
+        def _(hops):
+            ag_step(n - hops, hops)
+
+        rs_pair(n)
+
+    wa_hand_on()
+    wa_done()
+    scores[:, :dest_w] = jnp.zeros((rows, dest_w), F32)
+    add_source(t)
+
+    @pl.loop(heads, heads + n_tp - 1)
+    def _(n):
+        @pl.loop(jnp.maximum(n - n_tp + 1, 0), heads)
+        def _(h):
+            ag_step(h, n - h)
+
+        rs_pair(n)
+        hops = n - heads + 1
+
+        @pl.when(t >= hops)
+        def _():
+            add_source(t - hops)
+
+        @pl.when(t + hops < n_tp)
+        def _():
+            add_source(t + hops)
+
+    out_a[...] = scores[:, :dest_w].astype(BF16)
+    finish(out_h)
+
+    rim_copy().wait_send()
+    w_swap(w_hyena, me, 0).wait_send()
+    w_swap(w_far, flip, last).wait_send()
     w_flip().wait_send()
     for d in range(1, n_x):
         w_along(d, 0).wait_send()
@@ -444,15 +651,44 @@
     def _(step):
         m = step // GROUPS
         g = step % GROUPS
-        for layer in range(2):
-
-            @pl.when(t < n_tp - 1 - m)
-            def _():
-                rs_copy(layer, 0, n_tp - 1 - m, g).wait_send()
-
-            @pl.when(t > m)
-            def _():
-                rs_copy(layer, 1, m, g).wait_send()
+
+        @pl.when(t < n_tp - 1 - m)
+        def _():
+            rs_copy(0, n_tp - 1 - m, g).wait_send()
+
+        @pl.when(t > m)
+        def _():
+            rs_copy(1, m, g).wait_send()
+
+    for d in range(1, n_y):
+        wa_scatter(d).wait_send()
+        wa_up(d).wait_send()
+    for y_ in range(n_y):
+
+        @pl.when(2 * y_ + zh != t)
+        def _():
+            wa_line(y_).wait_send()
+
+    @pl.when(holder)
+    def _():
+        wa_flip().wait_send()
+
+    for d in range(1, n_x):
+        wa_along(d).wait_send()
+    for d in range(n_x):
+        wa_hand(d).wait_send()
+
+    @pl.loop(0, heads)
+    def _(h):
+        @pl.loop(0, n_tp)
+        def _(s):
+            @pl.when((s <= t) & (t < n_tp - 1))
+            def _():
+                ag_copy(h, 0, s).wait_send()
+
+            @pl.when((s >= t) & (t > 0))
+            def _():
+                ag_copy(h, 1, s).wait_send()
 
 
 def per_device(window, n_tp, hyena_in, filters, attn_in, out_weight, attn_weight):
@@ -468,7 +704,7 @@
     columns = piece * n_ctx
     dest_w = columns // n_tp
     heads = width // HEAD_DIM
-    n_w = 2 + 2 * n_x + 2 * n_y
+    n_w = 4 + 2 * n_x + 2 * n_y
     dma = pltpu.SemaphoreType.DMA
     result = jax.ShapeDtypeStruct((rows, dest_w), BF16)
     return pl.pallas_call(
@@ -478,11 +714,16 @@
         out_specs=(pl.BlockSpec(memory_space=pltpu.VMEM),) * 2,
         scratch_shapes=[
             pltpu.VMEM((2, slots, rows, width), BF16),
-            pltpu.VMEM((2, columns, width), BF16),
-            pltpu.VMEM((2, n_tp, rows, dest_w), BF16),
-            pltpu.VMEM((2, n_tp, rows, dest_w), BF16),
-            pltpu.VMEM((2, n_tp, rows, dest_w), BF16),
-            pltpu.VMEM((2, taps, width), BF16),
+            pltpu.VMEM((columns, width), BF16),
+            pltpu.VMEM((piece, width), BF16),
+            pltpu.VMEM((n_y, piece // n_y, width), BF16),
+            pltpu.VMEM((n_tp, dest_w, width), BF16),
+            pltpu.VMEM((n_tp, rows, width), BF16),
+            pltpu.VMEM((n_tp, rows, dest_w), BF16),
+            pltpu.VMEM((n_tp, rows, dest_w), BF16),
+            pltpu.VMEM((n_tp, rows, dest_w), BF16),
+            pltpu.VMEM((taps, width), BF16),
+            pltpu.VMEM((taps, width), BF16),
             pltpu.VMEM((taps + rows, width), F32),
             pltpu.VMEM((8, taps + rows, 128), F32),
             pltpu.VMEM((rows, width), BF16),
@@ -491,10 +732,14 @@
             dma((heads, 2 * n_x)),
             dma((n_w,)),
             dma((n_w,)),
-            dma((2, 2, n_tp, GROUPS)),
-            dma((2, 2, n_tp, GROUPS)),
-            dma((2,)),
-            dma((2,)),
+            dma((2, n_tp, GROUPS)),
+            dma((2, n_tp, GROUPS)),
+            dma,
+            dma,
+            dma((n_tp + 2 * n_y + 2 * n_x,)),
+            dma((3 * n_y + 2 * n_x,)),
+            dma((heads, n_tp)),
+            dma((heads, 2, n_tp)),
         ],
         compiler_params=pltpu.CompilerParams(
             collective_id=0, has_side_effects=True, vmem_limit_bytes=60 * 2**20

time: 232 us -> 177 us (0.76)
  the two profiles are of different devices: /device:TPU:96 before, /device:TPU:1 now
where the time goes in v2:
time: 177 us; the launch traced here: 176 us
  Pallas kernels  172 us (97%)
  local copies, waits for them, and re-layouts  2.42 us (1%)
    pallas_call x1, Pallas kernels, per_device(): pl.pallas_call(functools.partial(kernel, window), out_shape=(result, resu...  172 us

profile of v2, /device:TPU:1, one launch (start us, length us, event | category | flops | bytes accessed | tf_op | source)
XLA Modules:
  0.0 175.5 jit_solution(7912250821480468419)
XLA Ops:
  0.6 172.4 %shard_map.68 = (bf16[256,512]{1,0:T(8,128)(2,1)}, bf16[256,512]{1,0:T(8,128)(2,1)}) custom-call(bf16[3,256,512]{2,1,0:T(8,128)(2,1)} %bitcast.4, f32[128,512]{1,0:T(8,128)} %filters.1, bf16[3,256,512]{2,1,0:T(8,128)(2,1)} %bitcast.5, bf16[64,512]{1,0:T(8,128)(2,1)} %bitcast.6, bf16[64,512]{1,0:T(8,128)(2,1)} %bitcast.7), custom_call_target="tpu_custom_call" | custom-call | tf_op jit(solution)/shard_map/pallas_call | solution.py:710
  173.1 0.0 copy-start
  173.1 1.7 copy.9
  174.8 0.0 copy-done
  174.8 0.7 copy.10
Async XLA Ops:
  173.1 1.7 copy-start

commit v3 on v2

--- a/solution.py
+++ b/solution.py
@@ -429,25 +429,6 @@
 
         pass_on(h)
 
-    pltpu.make_async_copy(rim, rim, rim_recv).wait()
-    padded[pl.ds(0, taps), :] = jnp.where(me > 0, rim[...].astype(F32), 0.0)
-    convolve(0)
-    if chunk < taps:
-        convolve(chunk)
-
-    for d in range(n_y):
-        y_ = lax.rem(y + d, n_y)
-        w_landed(w_block(1 - k, y_ * 2 * slots, 2 * slots), base_p + d)
-
-    @pl.loop(0, n_tp)
-    def _(d):
-        weight = wg[pl.ds(pl.multiple_of(d * dest_w, dest_w), dest_w), :]
-        part[d] = lax.dot_general(
-            act[...], weight, (((1,), (1,)), ((), ())), preferred_element_type=F32
-        ).astype(BF16)
-
-    wa_spread()
-
     def rs_copy(way, d, g):
         piece_of = (d, pl.ds(pl.multiple_of(g * half, half), half))
         buffer = (from_left, from_right)[way]
@@ -466,27 +447,6 @@
         landed = buffer.at[piece_of]
         pltpu.make_async_copy(landed, landed, rs_recv.at[way, d, g]).wait()
         part[piece_of] = (part[piece_of].astype(F32) + buffer[piece_of].astype(F32)).astype(BF16)
-
-    def rs_way(way, tick):
-        hops = (t, n_tp - 1 - t)[way]
-        step = tick - hops
-        count = (n_tp - 1 - hops) * GROUPS
-        m = step // GROUPS
-        d = (n_tp - 1 - m, m)[way]
-        g = step % GROUPS
-        live = (step >= 0) & (step < count)
-
-        @pl.when(live & (hops > 0))
-        def _():
-            rs_add(way, d, g)
-
-        @pl.when(live)
-        def _():
-            rs_copy(way, d, g).start()
-
-    def rs_step(tick):
-        rs_way(0, tick)
-        rs_way(1, tick)
 
     rs_steps = (n_tp - 1) * GROUPS
 
@@ -553,76 +513,107 @@
             block, block, ag_send.at[h, way, s], ag_recv.at[h, s], (t + 1, t - 1)[way], "tp"
         )
 
-    def ag_step(h, hops):
-        for way in range(2):
-            s = (t - hops, t + hops)[way]
-            live = (s >= 0, s < n_tp)[way]
-            more = (t < n_tp - 1, t > 0)[way]
-
-            @pl.when(live & (hops > 0))
-            def _():
-                block = gathered.at[s, :, lanes(h)]
-                pltpu.make_async_copy(block, block, ag_recv.at[h, s]).wait()
-
-            @pl.when(live & more)
-            def _():
-                ag_copy(h, way, s).start()
+    def ag_own(h):
+        @pl.when(t < n_tp - 1)
+        def _():
+            ag_copy(h, 0, t).start()
+
+        @pl.when(t > 0)
+        def _():
+            ag_copy(h, 1, t).start()
+
+    def line_step(n):
+        for g in range(GROUPS):
+            for way in range(2):
+                ahead = (t, n_tp - 1 - t)[way]
+                more = ahead < n_tp - 1
+
+                @pl.when(n <= ahead)
+                def _():
+                    s = (t - n, t + n)[way]
+                    for h in range(g * heads // GROUPS, (g + 1) * heads // GROUPS):
+                        block = gathered.at[s, :, lanes(h)]
+                        pltpu.make_async_copy(block, block, ag_recv.at[h, s]).wait()
+
+                        @pl.when(more)
+                        def _():
+                            ag_copy(h, way, s).start()
+
+                @pl.when(n > ahead)
+                def _():
+                    m = n - ahead - 1
+                    d = (n_tp - 1 - m, m)[way]
+
+                    @pl.when(ahead > 0)
+                    def _():
+                        rs_add(way, d, g)
+
+                    rs_copy(way, d, g).start()
 
     def add_source(s):
         scores[:, :dest_w] += lax.dot_general(
             gathered[s], wa[s], (((1,), (1,)), ((), ())), preferred_element_type=F32
         )
 
-    def rs_pair(n):
-        @pl.loop(2 * n, jnp.minimum(2 * n + 2, rs_steps))
-        def _(tick):
-            rs_step(tick)
-
-    @pl.loop(0, heads // 2)
+    def add_sources(hops):
+        @pl.when(t >= hops)
+        def _():
+            add_source(t - hops)
+
+        @pl.when(t + hops < n_tp)
+        def _():
+            add_source(t + hops)
+
+    @pl.loop(0, heads)
+    def _(h):
+        rest(h)
+        attend(h)
+        ag_own(h)
+
+    pltpu.make_async_copy(rim, rim, rim_recv).wait()
+    padded[pl.ds(0, taps), :] = jnp.where(me > 0, rim[...].astype(F32), 0.0)
+    convolve(0)
+    if chunk < taps:
+        convolve(chunk)
+
+    for d in range(n_y):
+        y_ = lax.rem(y + d, n_y)
+        w_landed(w_block(1 - k, y_ * 2 * slots, 2 * slots), base_p + d)
+
+    @pl.loop(0, n_tp)
+    def _(d):
+        weight = wg[pl.ds(pl.multiple_of(d * dest_w, dest_w), dest_w), :]
+        part[d] = lax.dot_general(
+            act[...], weight, (((1,), (1,)), ((), ())), preferred_element_type=F32
+        ).astype(BF16)
+
+    wa_spread()
+    early = n_tp // 4 + 1
+    late = n_tp - n_tp // 4
+
+    @pl.loop(1, early)
     def _(n):
-        rest(n)
-        attend(n)
-
-        @pl.loop(0, n + 1)
-        def _(hops):
-            ag_step(n - hops, hops)
-
-        rs_pair(n)
+        line_step(n)
 
     wa_rows_done()
 
-    @pl.loop(heads // 2, heads)
+    @pl.loop(early, late)
     def _(n):
-        rest(n)
-        attend(n)
-
-        @pl.loop(0, n + 1)
-        def _(hops):
-            ag_step(n - hops, hops)
-
-        rs_pair(n)
+        line_step(n)
 
     wa_hand_on()
     wa_done()
     scores[:, :dest_w] = jnp.zeros((rows, dest_w), F32)
     add_source(t)
 
-    @pl.loop(heads, heads + n_tp - 1)
+    @pl.loop(1, late)
     def _(n):
-        @pl.loop(jnp.maximum(n - n_tp + 1, 0), heads)
-        def _(h):
-            ag_step(h, n - h)
-
-        rs_pair(n)
-        hops = n - heads + 1
-
-        @pl.when(t >= hops)
-        def _():
-            add_source(t - hops)
-
-        @pl.when(t + hops < n_tp)
-        def _():
-            add_source(t + hops)
+        add_sources(n)
+
+    @pl.loop(late, n_tp)
+    def _(n):
+        line_step(n)
+        add_sources(n)
 
     out_a[...] = scores[:, :dest_w].astype(BF16)
     finish(out_h)

time: 177 us -> 157 us (0.89)
  Pallas kernels: 172 us -> 153 us
    pallas_call x1, Pallas kernels: 172 us -> 153 us  [per_device(): pl.pallas_call(functools.partial(kernel, window), out_shape=(result, resu...]
where the time goes in v3:
time: 157 us; the launch traced here: 156 us
  Pallas kernels  153 us (97%)
  local copies, waits for them, and re-layouts  2.42 us (2%)
    pallas_call x1, Pallas kernels, per_device(): pl.pallas_call(functools.partial(kernel, window), out_shape=(result, resu...  153 us

profile of v3, /device:TPU:1, one launch (start us, length us, event | category | flops | bytes accessed | tf_op | source)
XLA Modules:
  0.0 156.2 jit_solution(13990965861485752930)
XLA Ops:
  0.6 153.1 %shard_map.68 = (bf16[256,512]{1,0:T(8,128)(2,1)}, bf16[256,512]{1,0:T(8,128)(2,1)}) custom-call(bf16[3,256,512]{2,1,0:T(8,128)(2,1)} %bitcast.4, f32[128,512]{1,0:T(8,128)} %filters.1, bf16[3,256,512]{2,1,0:T(8,128)(2,1)} %bitcast.5, bf16[64,512]{1,0:T(8,128)(2,1)} %bitcast.6, bf16[64,512]{1,0:T(8,128)(2,1)} %bitcast.7), custom_call_target="tpu_custom_call" | custom-call | tf_op jit(solution)/shard_map/pallas_call | solution.py:701
  153.8 0.0 copy-start
  153.8 1.7 %copy.9 = bf16[256,512]{1,0:T(8,128)(2,1)} copy(bf16[256,512]{1,0:T(8,128)(2,1)} %get-tuple-element.4) | data formatting | bytes 524288
  155.5 0.0 copy-done
  155.5 0.7 copy.10
Async XLA Ops:
  153.8 1.7 %copy-start = (bf16[256,512]{1,0:T(8,128)(2,1)S(1)}, bf16[256,512]{1,0:T(8,128)(2,1)}, u32[]{:S(2)}) copy-start(bf16[256,512]{1,0:T(8,128)(2,1)} %get-tuple-element.5) | copy-start | bytes 786436

commit v4 on v3

--- a/solution.py
+++ b/solution.py
@@ -407,28 +407,6 @@
     for d in range(1, n_y):
         w_up(d).start()
     w_hand(0).start()
-    spread(0)
-
-    @pl.loop(0, heads // 2)
-    def _(h):
-        spread(h + 1)
-        pass_on(h)
-
-    for d in range(1, n_y):
-        y_ = lax.rem(y + n_y - d, n_y)
-        w_landed(w_block(k, y_ * 2 * slots, 2 * slots), base_y + d)
-        w_hand(n_y - d).start()
-
-    wa_collect()
-
-    @pl.loop(heads // 2, heads)
-    def _(h):
-        @pl.when(h < heads - 1)
-        def _():
-            spread(h + 1)
-
-        pass_on(h)
-
     def rs_copy(way, d, g):
         piece_of = (d, pl.ds(pl.multiple_of(g * half, half), half))
         buffer = (from_left, from_right)[way]
@@ -564,18 +542,44 @@
         def _():
             add_source(t + hops)
 
-    @pl.loop(0, heads)
-    def _(h):
+    def turn(h):
         rest(h)
         attend(h)
         ag_own(h)
 
+    spread(0)
+
+    @pl.loop(0, heads // 2)
+    def _(h):
+        spread(h + 1)
+        pass_on(h)
+
+        @pl.when(h > 0)
+        def _():
+            turn(h - 1)
+
+    for d in range(1, n_y):
+        y_ = lax.rem(y + n_y - d, n_y)
+        w_landed(w_block(k, y_ * 2 * slots, 2 * slots), base_y + d)
+        w_hand(n_y - d).start()
+
+    wa_collect()
     pltpu.make_async_copy(rim, rim, rim_recv).wait()
     padded[pl.ds(0, taps), :] = jnp.where(me > 0, rim[...].astype(F32), 0.0)
     convolve(0)
     if chunk < taps:
         convolve(chunk)
 
+    @pl.loop(heads // 2, heads)
+    def _(h):
+        @pl.when(h < heads - 1)
+        def _():
+            spread(h + 1)
+
+        pass_on(h)
+        turn(h - 1)
+
+    turn(heads - 1)
     for d in range(n_y):
         y_ = lax.rem(y + d, n_y)
         w_landed(w_block(1 - k, y_ * 2 * slots, 2 * slots), base_p + d)
@@ -588,20 +592,21 @@
         ).astype(BF16)
 
     wa_spread()
-    early = n_tp // 4 + 1
-    late = n_tp - n_tp // 4
-
-    @pl.loop(1, early)
+    late = n_tp - 1
+
+    line_step(1)
+    wa_rows_done()
+
+    @pl.loop(2, late - 1)
     def _(n):
         line_step(n)
 
-    wa_rows_done()
-
-    @pl.loop(early, late)
+    wa_hand_on()
+
+    @pl.loop(max(late - 1, 2), late)
     def _(n):
         line_step(n)
 
-    wa_hand_on()
     wa_done()
     scores[:, :dest_w] = jnp.zeros((rows, dest_w), F32)
     add_source(t)
@@ -610,9 +615,12 @@
     def _(n):
         add_sources(n)
 
+    @pl.loop(max(late, 2), n_tp)
+    def _(n):
+        line_step(n)
+
     @pl.loop(late, n_tp)
     def _(n):
-        line_step(n)
         add_sources(n)
 
     out_a[...] = scores[:, :dest_w].astype(BF16)

time: 157 us -> 152 us (0.968)
  Pallas kernels: 153 us -> 149 us
    pallas_call x1, Pallas kernels: 153 us -> 149 us  [per_device(): pl.pallas_call(functools.partial(kernel, window), out_shape=(result, resu...]
where the time goes in v4:
time: 152 us
  Pallas kernels  149 us (98%)
  local copies, waits for them, and re-layouts  2.42 us (2%)
    pallas_call x1, Pallas kernels, per_device(): pl.pallas_call(functools.partial(kernel, window), out_shape=(result, resu...  149 us

profile of v4, /device:TPU:1, one launch (start us, length us, event | category | flops | bytes accessed | tf_op | source)
XLA Modules:
  0.0 151.9 jit_solution(3037947548402952066)
XLA Ops:
  0.6 148.8 %shard_map.68 = (bf16[256,512]{1,0:T(8,128)(2,1)}, bf16[256,512]{1,0:T(8,128)(2,1)}) custom-call(bf16[3,256,512]{2,1,0:T(8,128)(2,1)} %bitcast.4, f32[128,512]{1,0:T(8,128)} %filters.1, bf16[3,256,512]{2,1,0:T(8,128)(2,1)} %bitcast.5, bf16[64,512]{1,0:T(8,128)(2,1)} %bitcast.6, bf16[64,512]{1,0:T(8,128)(2,1)} %bitcast.7), custom_call_target="tpu_custom_call" | custom-call | tf_op jit(solution)/shard_map/pallas_call | solution.py:709
  149.5 0.0 copy-start
  149.5 1.7 %copy.9 = bf16[256,512]{1,0:T(8,128)(2,1)} copy(bf16[256,512]{1,0:T(8,128)(2,1)} %get-tuple-element.4) | data formatting | bytes 524288
  151.2 0.0 copy-done
  151.2 0.7 copy.10
Async XLA Ops:
  149.5 1.7 %copy-start = (bf16[256,512]{1,0:T(8,128)(2,1)S(1)}, bf16[256,512]{1,0:T(8,128)(2,1)}, u32[]{:S(2)}) copy-start(bf16[256,512]{1,0:T(8,128)(2,1)} %get-tuple-element.5) | copy-start | bytes 786436

commit v5 on v4

--- a/solution.py
+++ b/solution.py
@@ -597,35 +597,6 @@
     line_step(1)
     wa_rows_done()
 
-    @pl.loop(2, late - 1)
-    def _(n):
-        line_step(n)
-
-    wa_hand_on()
-
-    @pl.loop(max(late - 1, 2), late)
-    def _(n):
-        line_step(n)
-
-    wa_done()
-    scores[:, :dest_w] = jnp.zeros((rows, dest_w), F32)
-    add_source(t)
-
-    @pl.loop(1, late)
-    def _(n):
-        add_sources(n)
-
-    @pl.loop(max(late, 2), n_tp)
-    def _(n):
-        line_step(n)
-
-    @pl.loop(late, n_tp)
-    def _(n):
-        add_sources(n)
-
-    out_a[...] = scores[:, :dest_w].astype(BF16)
-    finish(out_h)
-
     rim_copy().wait_send()
     w_swap(w_hyena, me, 0).wait_send()
     w_swap(w_far, flip, last).wait_send()
@@ -646,18 +617,31 @@
             forward(h, d).wait_send()
         to_partner(h, own_kv(h)).wait_send()
 
-    @pl.loop(0, rs_steps)
-    def _(step):
-        m = step // GROUPS
-        g = step % GROUPS
-
-        @pl.when(t < n_tp - 1 - m)
-        def _():
-            rs_copy(0, n_tp - 1 - m, g).wait_send()
-
-        @pl.when(t > m)
-        def _():
-            rs_copy(1, m, g).wait_send()
+    @pl.loop(2, late - 1)
+    def _(n):
+        line_step(n)
+
+    wa_hand_on()
+
+    @pl.loop(max(late - 1, 2), late)
+    def _(n):
+        line_step(n)
+
+    wa_done()
+    scores[:, :dest_w] = jnp.zeros((rows, dest_w), F32)
+    add_source(t)
+
+    @pl.loop(1, late)
+    def _(n):
+        add_sources(n)
+
+    @pl.loop(max(late, 2), n_tp)
+    def _(n):
+        line_step(n)
+
+    @pl.loop(late, n_tp)
+    def _(n):
+        add_sources(n)
 
     for d in range(1, n_y):
         wa_scatter(d).wait_send()
@@ -688,6 +672,22 @@
             @pl.when((s >= t) & (t > 0))
             def _():
                 ag_copy(h, 1, s).wait_send()
+
+    out_a[...] = scores[:, :dest_w].astype(BF16)
+    finish(out_h)
+
+    @pl.loop(0, rs_steps)
+    def _(step):
+        m = step // GROUPS
+        g = step % GROUPS
+
+        @pl.when(t < n_tp - 1 - m)
+        def _():
+            rs_copy(0, n_tp - 1 - m, g).wait_send()
+
+        @pl.when(t > m)
+        def _():
+            rs_copy(1, m, g).wait_send()
 
 
 def per_device(window, n_tp, hyena_in, filters, attn_in, out_weight, attn_weight):

time: 152 us -> 152 us (level)
  no operation moved by 1% of the time
where the time goes in v5:
time: 152 us; the launch traced here: 151 us
  Pallas kernels  148 us (97%)
  local copies, waits for them, and re-layouts  2.42 us (2%)
    pallas_call x1, Pallas kernels, per_device(): pl.pallas_call(functools.partial(kernel, window), out_shape=(result, resu...  148 us

profile of v5, /device:TPU:1, one launch (start us, length us, event | category | flops | bytes accessed | tf_op | source)
XLA Modules:
  0.0 151.4 jit_solution(14874948577747867441)
XLA Ops:
  0.6 148.3 %shard_map.68 = (bf16[256,512]{1,0:T(8,128)(2,1)}, bf16[256,512]{1,0:T(8,128)(2,1)}) custom-call(bf16[3,256,512]{2,1,0:T(8,128)(2,1)} %bitcast.4, f32[128,512]{1,0:T(8,128)} %filters.1, bf16[3,256,512]{2,1,0:T(8,128)(2,1)} %bitcast.5, bf16[64,512]{1,0:T(8,128)(2,1)} %bitcast.6, bf16[64,512]{1,0:T(8,128)(2,1)} %bitcast.7), custom_call_target="tpu_custom_call" | custom-call | tf_op jit(solution)/shard_map/pallas_call | solution.py:709
  149.0 0.0 copy-start
  149.0 1.7 %copy.9 = bf16[256,512]{1,0:T(8,128)(2,1)} copy(bf16[256,512]{1,0:T(8,128)(2,1)} %get-tuple-element.4) | data formatting | bytes 524288
  150.7 0.0 copy-done
  150.7 0.7 copy.10
Async XLA Ops:
  149.0 1.7 %copy-start = (bf16[256,512]{1,0:T(8,128)(2,1)S(1)}, bf16[256,512]{1,0:T(8,128)(2,1)}, u32[]{:S(2)}) copy-start(bf16[256,512]{1,0:T(8,128)(2,1)} %get-tuple-element.5) | copy-start | bytes 786436
